TPU v7x, 32 devices: a whole 2x2x4 slice. The times are simulated.
32 devices in a mesh: clip: 4 (over x, core), tm: 8 (over z, y).
Axes of the slice: x: 2, y: 2, z: 4, core: 2. Of those that a mesh axis runs over, the one named last changes fastest.
Arguments:
- inputs: bfloat16 [4, 2560, 768], P('clip', 'tm'), may hold values from -6 to 6
- query_states: bfloat16 [4, 2560, 768], P('clip', 'tm'), may hold values from -9 to 9
- key_states: bfloat16 [4, 2560, 768], P('clip', 'tm'), may hold values from -9 to 9
- value_states: bfloat16 [4, 2560, 768], P('clip', 'tm'), may hold values from -6 to 6
- out_grad: bfloat16 [4, 2560, 768], P('clip', 'tm'), may hold values from -1.1953125 to 1.1953125
- first_flags: int32 [4, 8], P('clip'), may hold values from 0 to 1, as said below
- weight: float32 [768, 768], P('tm'), may hold values from -1.2 to 1.2
- moment_one: float32 [768, 768], P('tm'), may hold values from -6 to 6
- moment_two: float32 [768, 768], P('tm'), may hold values from 0.25 to 4
Outputs:
- new_weight: float32 [768, 768], P('tm')
- new_moment_one: float32 [768, 768], P('tm')
- new_moment_two: float32 [768, 768], P('tm')
Inputs may be any that keep to these rules, and one draw needn't show every extreme that they name: `first_flags`: the first frame of every sequence has flag 1.
All inputs are finite; a program needn't handle non-finite values.
Results may differ from a plain program's by a relative error of at most 0.0044.
Values may be sent and summed in bfloat16 or wider, within the bound.
No kernel may reach another device: no remote copies, remote signals or barrier semaphores. Data moves between devices by JAX's collectives and lax.ppermute only.
A program may use at most 64 MiB of HBM per device.

v0:
```python
import math
import jax
import jax.numpy as jnp
from jax import lax
from jax.sharding import PartitionSpec as P

HEAD_DIM = 128
beta_one = 0.9
beta_two = 0.95
learn_rate = 0.001
adam_eps = 1e-08
decay_rate = 0.1
step_count = 10.0


def from_behind(value, axis, steps):
    count = lax.axis_size(axis)
    leading, last = (max(0, -steps), min(count, count - steps))
    return lax.ppermute(value, axis, [(source, source + steps) for source in range(leading, last)])


def adamw(weight, moment_one, moment_two, gradient):
    new_one = beta_one * moment_one + (1.0 - beta_one) * gradient
    new_two = beta_two * moment_two + (1.0 - beta_two) * gradient * gradient
    corr_one = new_one / (1.0 - beta_one**step_count)
    corr_two = new_two / (1.0 - beta_two**step_count)
    new_weight = weight - learn_rate * (
        corr_one / (jnp.sqrt(corr_two) + adam_eps) + decay_rate * weight
    )
    return (new_weight, new_one, new_two)


def window_grad(query_rows, key_window, value_window, grad_rows, allowed):
    tok_rows = query_rows.shape[0]
    head_size = HEAD_DIM
    head_count = query_rows.shape[1] // head_size
    scaling = 1.0 / math.sqrt(head_size)
    query_heads = query_rows.reshape(tok_rows, head_count, head_size)
    key_heads = key_window.reshape(3 * tok_rows, head_count, head_size)
    value_heads = value_window.reshape(3 * tok_rows, head_count, head_size)
    grad_heads = grad_rows.reshape(tok_rows, head_count, head_size)
    scores = (
        jnp.einsum("qhd,khd->hqk", query_heads, key_heads, preferred_element_type=jnp.float32)
        * scaling
    )
    scores = jnp.where(allowed[None, None, :], scores, -jnp.inf)
    row_max = jnp.max(scores, axis=-1, keepdims=True)
    raised = jnp.exp(scores - row_max)
    softmax = raised / jnp.sum(raised, axis=-1, keepdims=True)
    dprobs = jnp.einsum("qhd,khd->hqk", grad_heads, value_heads, preferred_element_type=jnp.float32)
    row_dot = jnp.sum(softmax * dprobs, axis=-1, keepdims=True)
    dscores = (softmax * (dprobs - row_dot) * scaling).astype(jnp.bfloat16)
    window_part = jnp.einsum(
        "hqk,qhd->khd", dscores, query_heads, preferred_element_type=jnp.float32
    )
    return window_part.reshape(3 * tok_rows, head_count * head_size)


def contract_rows(features, key_grad):
    return lax.dot_general(
        features, key_grad, (((0,), (0,)), ((), ())), preferred_element_type=jnp.float32
    )


def body(
    inputs,
    query_states,
    key_states,
    value_states,
    out_grad,
    first_flags,
    weight,
    moment_one,
    moment_two,
):
    tok_rows = inputs.shape[1]
    position = lax.axis_index("tm")
    flag_row = first_flags[0]
    own_flag = flag_row[position]
    prev_flag = jnp.where(position >= 1, flag_row[jnp.maximum(position - 1, 0)], 1)
    near_ok = own_flag == 0
    far_ok = jnp.logical_and(near_ok, prev_flag == 0)
    allowed = jnp.concatenate(
        [
            jnp.broadcast_to(far_ok, (tok_rows,)),
            jnp.broadcast_to(near_ok, (tok_rows,)),
            jnp.ones((tok_rows,), bool),
        ]
    )
    queries = query_states[0]
    keys_own = key_states[0]
    values_own = value_states[0]
    near_keys, near_values = from_behind((keys_own, values_own), "tm", 1)
    far_keys, far_values = from_behind((keys_own, values_own), "tm", 2)
    key_window = jnp.concatenate([far_keys, near_keys, keys_own], axis=0)
    value_window = jnp.concatenate([far_values, near_values, values_own], axis=0)
    window_part = window_grad(queries, key_window, value_window, out_grad[0], allowed)
    far_part = window_part[:tok_rows]
    near_part = window_part[tok_rows : 2 * tok_rows]
    own_part = window_part[2 * tok_rows :]
    from_next = from_behind(near_part, "tm", -1)
    from_after = from_behind(far_part, "tm", -2)
    summed = own_part + from_next + from_after
    key_grad = summed.astype(jnp.bfloat16)
    features = inputs[0]
    local_rows = lax.psum_scatter(
        contract_rows(features, key_grad), "tm", scatter_dimension=0, tiled=True
    )
    gradient = lax.psum(local_rows, "clip")
    return adamw(weight, moment_one, moment_two, gradient)


def solution(mesh):
    in_specs = (
        P("clip", "tm", None),
        P("clip", "tm", None),
        P("clip", "tm", None),
        P("clip", "tm", None),
        P("clip", "tm", None),
        P("clip", None),
        P("tm", None),
        P("tm", None),
        P("tm", None),
    )
    out_specs = (P("tm", None), P("tm", None), P("tm", None))
    return jax.shard_map(body, mesh=mesh, in_specs=in_specs, out_specs=out_specs, check_vma=False)
```

profile of v0, /device:TPU:0, one launch (start us, length us, event | category | flops | bytes accessed | tf_op | source)
XLA Modules:
  0.0 265.4 jit_solution(16683940964910309810)
XLA Ops:
  7.2 5.9 %collective-permute-start = (bf16[320,768]{1,0:T(8,128)(2,1)}, bf16[320,768]{1,0:T(8,128)(2,1)}, u32[]{:S(2)}, u32[]{:S(2)}) collective-permute-start(bf16[320,768]{1,0:T(8,128)(2,1)} %bitcast.74), channel_id=1, source_target_pairs={{0,2},{1,3},{2,4},{3,5},{4,6},{5,7},{8,10},{9,11},{10,12},{11,13},... | collective-permute-start | bytes 1474568 | tf_op jit(solution)/shard_map/ppermute | solution.py:19
  13.1 4.2 %collective-permute-start.1 = (bf16[320,768]{1,0:T(8,128)(2,1)}, bf16[320,768]{1,0:T(8,128)(2,1)}, u32[]{:S(2)}, u32[]{:S(2)}) collective-permute-start(bf16[320,768]{1,0:T(8,128)(2,1)} %bitcast.75), channel_id=1, source_target_pairs={{0,1},{1,2},{2,3},{3,4},{4,5},{5,6},{6,7},{8,9},{9,10},{10,11},{11... | collective-permute-start | bytes 1474568 | tf_op jit(solution)/shard_map/ppermute | solution.py:19
  17.3 2.7 %collective-permute-start.2 = (bf16[320,768]{1,0:T(8,128)(2,1)}, bf16[320,768]{1,0:T(8,128)(2,1)}, u32[]{:S(2)}, u32[]{:S(2)}) collective-permute-start(bf16[320,768]{1,0:T(8,128)(2,1)} %bitcast.76), channel_id=1, source_target_pairs={{0,2},{1,3},{2,4},{3,5},{4,6},{5,7},{8,10},{9,11},{10,12},{11,13},... | collective-permute-start | bytes 1474568 | tf_op jit(solution)/shard_map/ppermute | solution.py:19
  20.0 4.2 %collective-permute-start.3 = (bf16[320,768]{1,0:T(8,128)(2,1)}, bf16[320,768]{1,0:T(8,128)(2,1)}, u32[]{:S(2)}, u32[]{:S(2)}) collective-permute-start(bf16[320,768]{1,0:T(8,128)(2,1)} %bitcast.77), channel_id=1, source_target_pairs={{0,1},{1,2},{2,3},{3,4},{4,5},{5,6},{6,7},{8,9},{9,10},{10,11},{11... | collective-permute-start | bytes 1474568 | tf_op jit(solution)/shard_map/ppermute | solution.py:19
  25.6 1.3 copy.90
  28.9 1.3 copy.86
  30.9 1.3 copy.94
  42.5 5.6 %fusion.21 = f32[6,960,320]{1,2,0:T(8,128)} fusion(bf16[320,6,128]{0,2,1:T(8,128)(2,1)S(1)} %bitcast.65, bf16[320,6,128]{2,0,1:T(8,128)(2,1)S(1)} %copy.85, bf16[320,6,128]{2,0,1:T(8,128)(2,1)} %copy.84, bf16[320,6,128]{2,0,1:T(8,128)(2,1)} %copy.83), kind=kOutput, calls=%fused_computation.22 | convolution fusion | flops 476282880 | bytes 9338880 | tf_op jit(solution)/shard_map/qhd,khd->hqk/dot_general | solution.py:43
  48.1 11.5 %fusion.16 = f32[6,320,960]{2,1,0:T(8,128)} fusion(f32[6,960,320]{1,2,0:T(8,128)} %fusion.21, pred[960]{0:T(1024)(128)(4,1)S(1)} %pad_add_fusion), kind=kOutput, calls=%fused_computation.18 | output fusion | flops 11064958 | bytes 14746560 | tf_op jit(solution)/shard_map/div | solution.py:49
  59.6 4.4 %fusion.27 = f32[6,960,320]{1,2,0:T(8,128)} fusion(bf16[320,6,128]{0,2,1:T(8,128)(2,1)S(1)} %bitcast.67, bf16[320,6,128]{2,0,1:T(8,128)(2,1)S(1)} %copy.93, bf16[320,6,128]{2,0,1:T(8,128)(2,1)S(1)} %copy-done.2, bf16[320,6,128]{2,0,1:T(8,128)(2,1)S(1)} %copy-done.1), kind=kOutput, calls=%fused_computation.28 | convolution fusion | flops 476282880 | bytes 9338880 | tf_op jit(solution)/shard_map/qhd,khd->hqk/dot_general | solution.py:50
  64.0 14.1 %fusion.18 = f32[960,6,128]{2,0,1:T(8,128)} fusion(bf16[320,6,128]{0,2,1:T(8,128)(2,1)S(1)} %bitcast.66, f32[6,320,960]{2,1,0:T(8,128)} %fusion.16, f32[6,960,320]{1,2,0:T(8,128)} %fusion.27), kind=kOutput, calls=%fused_computation.20 | convolution fusion | flops 481078080 | bytes 18186240 | tf_op jit(solution)/shard_map/hqk,qhd->khd/dot_general | solution.py:53
  78.0 3.3 %fusion.44 = (f32[320,6,128]{2,0,1:T(8,128)S(1)}, f32[320,6,128]{2,0,1:T(8,128)}, f32[320,6,128]{2,0,1:T(8,128)}) fusion(f32[960,6,128]{2,0,1:T(8,128)} %fusion.18), kind=kLoop, calls=%fused_computation.51 | loop fusion | bytes 5898240 | tf_op jit(solution)/shard_map/slice | solution.py:100
  81.3 1.6 copy.98
  82.9 1.5 copy.99
  85.7 1.6 copy.101
  90.2 33.4 %collective-permute-done.4 = f32[320,768]{1,0:T(8,128)} collective-permute-done((f32[320,768]{1,0:T(8,128)}, f32[320,768]{1,0:T(8,128)}, u32[]{:S(2)}, u32[]{:S(2)}) %collective-permute-start.4) | collective-permute-done | bytes 983072 | tf_op jit(solution)/shard_map/ppermute | solution.py:19
  123.6 1.6 copy.100
  125.2 21.4 %collective-permute-done.5 = f32[320,768]{1,0:T(8,128)} collective-permute-done((f32[320,768]{1,0:T(8,128)}, f32[320,768]{1,0:T(8,128)}, u32[]{:S(2)}, u32[]{:S(2)}) %collective-permute-start.5) | collective-permute-done | bytes 983072 | tf_op jit(solution)/shard_map/ppermute | solution.py:19
  146.6 2.6 copy.103
  149.2 1.4 fusion.34
  151.4 2.0 copy.108
  153.5 69.0 %reduce-scatter.4.cloned.1.call-done = f32[96,768]{1,0:T(8,128)} async-done(((f32[768,768]{1,0:T(8,128)}), f32[96,768]{1,0:T(8,128)}) %reduce-scatter.4.cloned.1.call-update) | async-done | bytes 294928 | tf_op jit(solution)/shard_map/reduce_scatter | solution.py:106
  222.5 33.9 %all-reduce.2.cloned.1.call-done = f32[96,768]{1,0:T(8,128)} async-done(((f32[96,768]{1,0:T(8,128)}), f32[96,768]{1,0:T(8,128)}) %all-reduce.2.cloned.1.call-update) | async-done | bytes 294928 | tf_op jit(solution)/shard_map/psum | solution.py:109
  256.4 2.1 multiply_subtract_fusion
  (39 shorter events, 18.0 us)
Async XLA Ops:
  7.2 143.5 %copy-start = (bf16[1,320,768]{2,1,0:T(8,128)(2,1)S(1)}, bf16[1,320,768]{2,1,0:T(8,128)(2,1)}, u32[]{:S(2)}) copy-start(bf16[1,320,768]{2,1,0:T(8,128)(2,1)} %param.9) | copy-start | bytes 1474564
  7.2 215.3 %reduce-scatter.4.cloned.1.call-start = ((), (), s32[]{:S(2)}) async-start(), calls=%async_computation.2 | async-start | bytes 2654208 | tf_op jit(solution)/shard_map/reduce_scatter | solution.py:106
  7.2 25.8 %collective-permute-start = (bf16[320,768]{1,0:T(8,128)(2,1)}, bf16[320,768]{1,0:T(8,128)(2,1)}, u32[]{:S(2)}, u32[]{:S(2)}) collective-permute-start(bf16[320,768]{1,0:T(8,128)(2,1)} %bitcast.74), channel_id=1, source_target_pairs={{0,2},{1,3},{2,4},{3,5},{4,6},{5,7},{8,10},{9,11},{10,12},{11,13},... | collective-permute-start | bytes 1474568 | tf_op jit(solution)/shard_map/ppermute | solution.py:19
  13.1 22.3 %collective-permute-start.1 = (bf16[320,768]{1,0:T(8,128)(2,1)}, bf16[320,768]{1,0:T(8,128)(2,1)}, u32[]{:S(2)}, u32[]{:S(2)}) collective-permute-start(bf16[320,768]{1,0:T(8,128)(2,1)} %bitcast.75), channel_id=1, source_target_pairs={{0,1},{1,2},{2,3},{3,4},{4,5},{5,6},{6,7},{8,9},{9,10},{10,11},{11... | collective-permute-start | bytes 1474568 | tf_op jit(solution)/shard_map/ppermute | solution.py:19
  17.3 20.4 %collective-permute-start.2 = (bf16[320,768]{1,0:T(8,128)(2,1)}, bf16[320,768]{1,0:T(8,128)(2,1)}, u32[]{:S(2)}, u32[]{:S(2)}) collective-permute-start(bf16[320,768]{1,0:T(8,128)(2,1)} %bitcast.76), channel_id=1, source_target_pairs={{0,2},{1,3},{2,4},{3,5},{4,6},{5,7},{8,10},{9,11},{10,12},{11,13},... | collective-permute-start | bytes 1474568 | tf_op jit(solution)/shard_map/ppermute | solution.py:19
  20.0 20.1 %collective-permute-start.3 = (bf16[320,768]{1,0:T(8,128)(2,1)}, bf16[320,768]{1,0:T(8,128)(2,1)}, u32[]{:S(2)}, u32[]{:S(2)}) collective-permute-start(bf16[320,768]{1,0:T(8,128)(2,1)} %bitcast.77), channel_id=1, source_target_pairs={{0,1},{1,2},{2,3},{3,4},{4,5},{5,6},{6,7},{8,9},{9,10},{10,11},{11... | collective-permute-start | bytes 1474568 | tf_op jit(solution)/shard_map/ppermute | solution.py:19
  48.1 11.5 %copy-start.1 = (bf16[320,6,128]{2,0,1:T(8,128)(2,1)S(1)}, bf16[320,6,128]{2,0,1:T(8,128)(2,1)}, u32[]{:S(2)}) copy-start(bf16[320,6,128]{2,0,1:T(8,128)(2,1)} %copy.91) | copy-start | bytes 1474564
  48.1 11.5 %copy-start.2 = (bf16[320,6,128]{2,0,1:T(8,128)(2,1)S(1)}, bf16[320,6,128]{2,0,1:T(8,128)(2,1)}, u32[]{:S(2)}) copy-start(bf16[320,6,128]{2,0,1:T(8,128)(2,1)} %copy.92) | copy-start | bytes 1474564
  84.4 39.2 %collective-permute-start.4 = (f32[320,768]{1,0:T(8,128)}, f32[320,768]{1,0:T(8,128)}, u32[]{:S(2)}, u32[]{:S(2)}) collective-permute-start(f32[320,768]{1,0:T(8,128)} %copy.99), channel_id=1, source_target_pairs={{1,0},{2,1},{3,2},{4,3},{5,4},{6,5},{7,6},{9,8},{10,9},{11,10},{12... | collective-permute-start | bytes 2949128 | tf_op jit(solution)/shard_map/ppermute | solution.py:19
  88.6 58.0 %collective-permute-start.5 = (f32[320,768]{1,0:T(8,128)}, f32[320,768]{1,0:T(8,128)}, u32[]{:S(2)}, u32[]{:S(2)}) collective-permute-start(f32[320,768]{1,0:T(8,128)} %copy.102), channel_id=1, source_target_pairs={{2,0},{3,1},{4,2},{5,3},{6,4},{7,5},{10,8},{11,9},{12,10},{13,11},... | collective-permute-start | bytes 2949128 | tf_op jit(solution)/shard_map/ppermute | solution.py:19
  151.4 105.0 %copy-start.3 = (f32[96,768]{1,0:T(8,128)S(1)}, f32[96,768]{1,0:T(8,128)}, u32[]{:S(2)}) copy-start(f32[96,768]{1,0:T(8,128)} %param.15) | copy-start | bytes 884740
  151.4 105.0 %copy-start.4 = (f32[96,768]{1,0:T(8,128)S(1)}, f32[96,768]{1,0:T(8,128)}, u32[]{:S(2)}) copy-start(f32[96,768]{1,0:T(8,128)} %param.16) | copy-start | bytes 884740
  153.4 103.0 %all-reduce.2.cloned.1.call-start = ((), (), s32[]{:S(2)}) async-start(), calls=%async_computation.1 | async-start | bytes 589824 | tf_op jit(solution)/shard_map/psum | solution.py:109
Sparse Core Ops, SparseCore 0:
  153.5 68.8 reduce-scatter.3
  224.8 31.5 all-reduce.1
where the time goes:
time: 266 us; the launch traced here: 265 us
  waiting for transfers between devices  158 us (59%)
  local copies, waits for them, and re-layouts  32.5 us (12%)
  matrix products  24.8 us (9%)
  starting transfers between devices  19.7 us (7%)
  between operations  15.5 us (6%)
  other arithmetic  15.1 us (6%)
    reduce_scatter x1, waiting for transfers between devices, body(): lax.psum_scatter(contract_rows(features, key_grad), 'tm', scatter_dimensi...  69 us
    ppermute x6, waiting for transfers between devices, from_behind(): lax.ppermute(value, axis, [(source, source + steps) for source in range(l...  54.8 us
    psum x1, waiting for transfers between devices, body(): gradient = lax.psum(local_rows, 'clip')  33.9 us
    ppermute x6, starting transfers between devices, from_behind(): lax.ppermute(value, axis, [(source, source + steps) for source in range(l...  19.6 us
    dot_general x1, matrix products, window_grad(): jnp.einsum('hqk,qhd->khd', dscores, query_heads, preferred_element_type=j...  14.1 us
    div x1, other arithmetic, window_grad(): softmax = raised / jnp.sum(raised, axis=-1, keepdims=True)  11.5 us
    ppermute x6, local copies, waits for them, and re-layouts, from_behind(): lax.ppermute(value, axis, [(source, source + steps) for source in range(l...  9.48 us
    unnamed x15, local copies, waits for them, and re-layouts  7.34 us
  transfers between devices with their start and end apart: 8, of which 4 were waited for; matrix products, arithmetic and copies ran while one was open for 7% of the time, Pallas kernels for 0%

commit v1 on v0

--- a/solution.py
+++ b/solution.py
@@ -106,7 +106,7 @@
     local_rows = lax.psum_scatter(
         contract_rows(features, key_grad), "tm", scatter_dimension=0, tiled=True
     )
-    gradient = lax.psum(local_rows, "clip")
+    gradient = jnp.sum(lax.all_gather(local_rows, "clip"), axis=0)
     return adamw(weight, moment_one, moment_two, gradient)
 
 

time: 266 us -> 251 us (0.944)
  waiting for transfers between devices: 158 us -> 142 us
    psum x1 -> x0, waiting for transfers between devices: 33.9 us -> none  [body(): gradient = lax.psum(local_rows, 'clip')]
    all_gather x0 -> x1, waiting for transfers between devices: none -> 18.2 us  [body(): gradient = jnp.sum(lax.all_gather(local_rows, 'clip'), axis=0)]
    unnamed x15 -> x17, local copies, waits for them, and re-layouts: 7.34 us -> 7.33 us
  transfers between devices with their start and end apart: 8 -> 8, of which waited for: 4 -> 4; matrix products, arithmetic and copies ran while one was open for 7% -> 8% of each run, Pallas kernels for 0% -> 0%
where the time goes in v1:
time: 251 us; the launch traced here: 250 us
  waiting for transfers between devices  142 us (57%)
  local copies, waits for them, and re-layouts  32.5 us (13%)
  matrix products  24.8 us (10%)
  starting transfers between devices  19.7 us (8%)
  between operations  15.5 us (6%)
  other arithmetic  15.4 us (6%)
    reduce_scatter x1, waiting for transfers between devices, body(): lax.psum_scatter(contract_rows(features, key_grad), 'tm', scatter_dimensi...  69.2 us
    ppermute x6, waiting for transfers between devices, from_behind(): lax.ppermute(value, axis, [(source, source + steps) for source in range(l...  54.8 us
    ppermute x6, starting transfers between devices, from_behind(): lax.ppermute(value, axis, [(source, source + steps) for source in range(l...  19.6 us
    all_gather x1, waiting for transfers between devices, body(): gradient = jnp.sum(lax.all_gather(local_rows, 'clip'), axis=0)  18.2 us
    dot_general x1, matrix products, window_grad(): jnp.einsum('hqk,qhd->khd', dscores, query_heads, preferred_element_type=j...  14.1 us
    div x1, other arithmetic, window_grad(): softmax = raised / jnp.sum(raised, axis=-1, keepdims=True)  11.5 us
    ppermute x6, local copies, waits for them, and re-layouts, from_behind(): lax.ppermute(value, axis, [(source, source + steps) for source in range(l...  9.48 us
    unnamed x17, local copies, waits for them, and re-layouts  7.33 us
  transfers between devices with their start and end apart: 8, of which 4 were waited for; matrix products, arithmetic and copies ran while one was open for 8% of the time, Pallas kernels for 0%

profile of v1, /device:TPU:0, one launch (start us, length us, event | category | flops | bytes accessed | tf_op | source)
XLA Modules:
  0.0 250.1 jit_solution(7545622890301986368)
XLA Ops:
  7.2 5.9 %collective-permute-start = (bf16[320,768]{1,0:T(8,128)(2,1)}, bf16[320,768]{1,0:T(8,128)(2,1)}, u32[]{:S(2)}, u32[]{:S(2)}) collective-permute-start(bf16[320,768]{1,0:T(8,128)(2,1)} %bitcast.76), channel_id=1, source_target_pairs={{0,2},{1,3},{2,4},{3,5},{4,6},{5,7},{8,10},{9,11},{10,12},{11,13},... | collective-permute-start | bytes 1474568 | tf_op jit(solution)/shard_map/ppermute | solution.py:19
  13.1 4.2 %collective-permute-start.1 = (bf16[320,768]{1,0:T(8,128)(2,1)}, bf16[320,768]{1,0:T(8,128)(2,1)}, u32[]{:S(2)}, u32[]{:S(2)}) collective-permute-start(bf16[320,768]{1,0:T(8,128)(2,1)} %bitcast.77), channel_id=1, source_target_pairs={{0,1},{1,2},{2,3},{3,4},{4,5},{5,6},{6,7},{8,9},{9,10},{10,11},{11... | collective-permute-start | bytes 1474568 | tf_op jit(solution)/shard_map/ppermute | solution.py:19
  17.3 2.8 %collective-permute-start.2 = (bf16[320,768]{1,0:T(8,128)(2,1)}, bf16[320,768]{1,0:T(8,128)(2,1)}, u32[]{:S(2)}, u32[]{:S(2)}) collective-permute-start(bf16[320,768]{1,0:T(8,128)(2,1)} %bitcast.78), channel_id=1, source_target_pairs={{0,2},{1,3},{2,4},{3,5},{4,6},{5,7},{8,10},{9,11},{10,12},{11,13},... | collective-permute-start | bytes 1474568 | tf_op jit(solution)/shard_map/ppermute | solution.py:19
  20.0 4.2 %collective-permute-start.3 = (bf16[320,768]{1,0:T(8,128)(2,1)}, bf16[320,768]{1,0:T(8,128)(2,1)}, u32[]{:S(2)}, u32[]{:S(2)}) collective-permute-start(bf16[320,768]{1,0:T(8,128)(2,1)} %bitcast.79), channel_id=1, source_target_pairs={{0,1},{1,2},{2,3},{3,4},{4,5},{5,6},{6,7},{8,9},{9,10},{10,11},{11... | collective-permute-start | bytes 1474568 | tf_op jit(solution)/shard_map/ppermute | solution.py:19
  25.6 1.3 copy.46
  28.9 1.3 copy.42
  30.9 1.3 copy.50
  42.5 5.6 %fusion.21 = f32[6,960,320]{1,2,0:T(8,128)} fusion(bf16[320,6,128]{0,2,1:T(8,128)(2,1)S(1)} %bitcast.66, bf16[320,6,128]{2,0,1:T(8,128)(2,1)S(1)} %copy.41, bf16[320,6,128]{2,0,1:T(8,128)(2,1)} %copy.40, bf16[320,6,128]{2,0,1:T(8,128)(2,1)} %copy.39), kind=kOutput, calls=%fused_computation.22 | convolution fusion | flops 476282880 | bytes 9338880 | tf_op jit(solution)/shard_map/qhd,khd->hqk/dot_general | solution.py:43
  48.1 11.5 %fusion.16 = f32[6,320,960]{2,1,0:T(8,128)} fusion(f32[6,960,320]{1,2,0:T(8,128)} %fusion.21, pred[960]{0:T(1024)(128)(4,1)S(1)} %pad_add_fusion), kind=kOutput, calls=%fused_computation.18 | output fusion | flops 11064958 | bytes 14746560 | tf_op jit(solution)/shard_map/div | solution.py:49
  59.6 4.4 %fusion.27 = f32[6,960,320]{1,2,0:T(8,128)} fusion(bf16[320,6,128]{0,2,1:T(8,128)(2,1)S(1)} %bitcast.68, bf16[320,6,128]{2,0,1:T(8,128)(2,1)S(1)} %copy.49, bf16[320,6,128]{2,0,1:T(8,128)(2,1)S(1)} %copy-done.2, bf16[320,6,128]{2,0,1:T(8,128)(2,1)S(1)} %copy-done.1), kind=kOutput, calls=%fused_computation.28 | convolution fusion | flops 476282880 | bytes 9338880 | tf_op jit(solution)/shard_map/qhd,khd->hqk/dot_general | solution.py:50
  64.0 14.1 %fusion.18 = f32[960,6,128]{2,0,1:T(8,128)} fusion(bf16[320,6,128]{0,2,1:T(8,128)(2,1)S(1)} %bitcast.67, f32[6,320,960]{2,1,0:T(8,128)} %fusion.16, f32[6,960,320]{1,2,0:T(8,128)} %fusion.27), kind=kOutput, calls=%fused_computation.20 | convolution fusion | flops 481078080 | bytes 18186240 | tf_op jit(solution)/shard_map/hqk,qhd->khd/dot_general | solution.py:53
  78.0 3.3 %fusion.44 = (f32[320,6,128]{2,0,1:T(8,128)S(1)}, f32[320,6,128]{2,0,1:T(8,128)}, f32[320,6,128]{2,0,1:T(8,128)}) fusion(f32[960,6,128]{2,0,1:T(8,128)} %fusion.18), kind=kLoop, calls=%fused_computation.51 | loop fusion | bytes 5898240 | tf_op jit(solution)/shard_map/slice | solution.py:100
  81.4 1.6 copy.54
  82.9 1.5 copy.55
  85.7 1.6 copy.57
  90.3 33.3 %collective-permute-done.4 = f32[320,768]{1,0:T(8,128)} collective-permute-done((f32[320,768]{1,0:T(8,128)}, f32[320,768]{1,0:T(8,128)}, u32[]{:S(2)}, u32[]{:S(2)}) %collective-permute-start.4) | collective-permute-done | bytes 983072 | tf_op jit(solution)/shard_map/ppermute | solution.py:19
  123.6 1.6 copy.56
  125.2 21.4 %collective-permute-done.5 = f32[320,768]{1,0:T(8,128)} collective-permute-done((f32[320,768]{1,0:T(8,128)}, f32[320,768]{1,0:T(8,128)}, u32[]{:S(2)}, u32[]{:S(2)}) %collective-permute-start.5) | collective-permute-done | bytes 983072 | tf_op jit(solution)/shard_map/ppermute | solution.py:19
  146.6 2.6 %copy.59 = f32[320,768]{0,1:T(8,128)} copy(f32[320,768]{1,0:T(8,128)} %collective-permute-done.5) | data formatting | bytes 1966080 | tf_op jit(solution)/shard_map/ppermute | solution.py:19
  149.2 1.4 fusion.34
  151.4 2.0 copy.64
  153.4 69.2 %reduce-scatter.4.cloned.1.call-done = f32[96,768]{1,0:T(8,128)} async-done(((f32[768,768]{1,0:T(8,128)}), f32[96,768]{1,0:T(8,128)}) %reduce-scatter.4.cloned.1.call-update) | async-done | bytes 294928 | tf_op jit(solution)/shard_map/reduce_scatter | solution.py:106
  222.6 18.2 %all-gather.3.cloned.1.call-done = f32[384,768]{1,0:T(8,128)} async-done(((f32[96,768]{1,0:T(8,128)}), f32[384,768]{1,0:T(8,128)}) %all-gather.3.cloned.1.call-update) | async-done | bytes 1179664 | tf_op jit(solution)/shard_map/all_gather | solution.py:109
  240.9 1.4 reduce_sum.29
  (42 shorter events, 19.0 us)
Async XLA Ops:
  7.2 143.5 %copy-start = (bf16[1,320,768]{2,1,0:T(8,128)(2,1)S(1)}, bf16[1,320,768]{2,1,0:T(8,128)(2,1)}, u32[]{:S(2)}) copy-start(bf16[1,320,768]{2,1,0:T(8,128)(2,1)} %param.9) | copy-start | bytes 1474564
  7.2 215.4 %reduce-scatter.4.cloned.1.call-start = ((), (), s32[]{:S(2)}) async-start(), calls=%async_computation.2 | async-start | bytes 2654208 | tf_op jit(solution)/shard_map/reduce_scatter | solution.py:106
  7.2 25.8 %collective-permute-start = (bf16[320,768]{1,0:T(8,128)(2,1)}, bf16[320,768]{1,0:T(8,128)(2,1)}, u32[]{:S(2)}, u32[]{:S(2)}) collective-permute-start(bf16[320,768]{1,0:T(8,128)(2,1)} %bitcast.76), channel_id=1, source_target_pairs={{0,2},{1,3},{2,4},{3,5},{4,6},{5,7},{8,10},{9,11},{10,12},{11,13},... | collective-permute-start | bytes 1474568 | tf_op jit(solution)/shard_map/ppermute | solution.py:19
  13.1 22.3 %collective-permute-start.1 = (bf16[320,768]{1,0:T(8,128)(2,1)}, bf16[320,768]{1,0:T(8,128)(2,1)}, u32[]{:S(2)}, u32[]{:S(2)}) collective-permute-start(bf16[320,768]{1,0:T(8,128)(2,1)} %bitcast.77), channel_id=1, source_target_pairs={{0,1},{1,2},{2,3},{3,4},{4,5},{5,6},{6,7},{8,9},{9,10},{10,11},{11... | collective-permute-start | bytes 1474568 | tf_op jit(solution)/shard_map/ppermute | solution.py:19
  17.3 20.5 %collective-permute-start.2 = (bf16[320,768]{1,0:T(8,128)(2,1)}, bf16[320,768]{1,0:T(8,128)(2,1)}, u32[]{:S(2)}, u32[]{:S(2)}) collective-permute-start(bf16[320,768]{1,0:T(8,128)(2,1)} %bitcast.78), channel_id=1, source_target_pairs={{0,2},{1,3},{2,4},{3,5},{4,6},{5,7},{8,10},{9,11},{10,12},{11,13},... | collective-permute-start | bytes 1474568 | tf_op jit(solution)/shard_map/ppermute | solution.py:19
  20.0 20.1 %collective-permute-start.3 = (bf16[320,768]{1,0:T(8,128)(2,1)}, bf16[320,768]{1,0:T(8,128)(2,1)}, u32[]{:S(2)}, u32[]{:S(2)}) collective-permute-start(bf16[320,768]{1,0:T(8,128)(2,1)} %bitcast.79), channel_id=1, source_target_pairs={{0,1},{1,2},{2,3},{3,4},{4,5},{5,6},{6,7},{8,9},{9,10},{10,11},{11... | collective-permute-start | bytes 1474568 | tf_op jit(solution)/shard_map/ppermute | solution.py:19
  48.1 11.5 %copy-start.1 = (bf16[320,6,128]{2,0,1:T(8,128)(2,1)S(1)}, bf16[320,6,128]{2,0,1:T(8,128)(2,1)}, u32[]{:S(2)}) copy-start(bf16[320,6,128]{2,0,1:T(8,128)(2,1)} %copy.47) | copy-start | bytes 1474564
  48.1 11.5 %copy-start.2 = (bf16[320,6,128]{2,0,1:T(8,128)(2,1)S(1)}, bf16[320,6,128]{2,0,1:T(8,128)(2,1)}, u32[]{:S(2)}) copy-start(bf16[320,6,128]{2,0,1:T(8,128)(2,1)} %copy.48) | copy-start | bytes 1474564
  84.4 39.2 %collective-permute-start.4 = (f32[320,768]{1,0:T(8,128)}, f32[320,768]{1,0:T(8,128)}, u32[]{:S(2)}, u32[]{:S(2)}) collective-permute-start(f32[320,768]{1,0:T(8,128)} %copy.55), channel_id=1, source_target_pairs={{1,0},{2,1},{3,2},{4,3},{5,4},{6,5},{7,6},{9,8},{10,9},{11,10},{12... | collective-permute-start | bytes 2949128 | tf_op jit(solution)/shard_map/ppermute | solution.py:19
  88.6 58.0 %collective-permute-start.5 = (f32[320,768]{1,0:T(8,128)}, f32[320,768]{1,0:T(8,128)}, u32[]{:S(2)}, u32[]{:S(2)}) collective-permute-start(f32[320,768]{1,0:T(8,128)} %copy.58), channel_id=1, source_target_pairs={{2,0},{3,1},{4,2},{5,3},{6,4},{7,5},{10,8},{11,9},{12,10},{13,11},... | collective-permute-start | bytes 2949128 | tf_op jit(solution)/shard_map/ppermute | solution.py:19
  153.4 88.9 %copy-start.3 = (f32[96,768]{1,0:T(8,128)S(1)}, f32[96,768]{1,0:T(8,128)}, u32[]{:S(2)}) copy-start(f32[96,768]{1,0:T(8,128)} %param.15) | copy-start | bytes 884740
  153.4 88.9 %copy-start.4 = (f32[96,768]{1,0:T(8,128)S(1)}, f32[96,768]{1,0:T(8,128)}, u32[]{:S(2)}) copy-start(f32[96,768]{1,0:T(8,128)} %param.16) | copy-start | bytes 884740
  153.4 88.9 %copy-start.5 = (f32[96,768]{1,0:T(8,128)S(1)}, f32[96,768]{1,0:T(8,128)}, u32[]{:S(2)}) copy-start(f32[96,768]{1,0:T(8,128)} %param.17) | copy-start | bytes 884740
  153.4 87.5 %all-gather.3.cloned.1.call-start = ((), (), s32[]{:S(2)}) async-start(), calls=%async_computation.1 | async-start | bytes 1474560 | tf_op jit(solution)/shard_map/all_gather | solution.py:109
Sparse Core Ops, SparseCore 0:
  153.5 69.0 reduce-scatter.3
  224.2 16.6 all-gather.2
